TPU v7x, 256 devices: a whole 4x4x8 slice. The times are simulated.
256 devices in a mesh: row: 32 (over y, x, core), col: 8 (over z).
Axes of the slice: x: 4, y: 4, z: 8, core: 2. Of those that a mesh axis runs over, the one named last changes fastest.
Arguments:
- distances: float32 [12288, 12288], P('row', 'col'), may hold values from 0 to 4096, as said below
Outputs:
- shortest: float32 [12288, 12288], P('row', 'col')
Inputs may be any that keep to these rules, and one draw needn't show every extreme that they name: `distances`: every off-diagonal entry is a whole number from 1 to 64 or the no-edge value 4096; every diagonal entry is 0.
All inputs are finite; a program needn't handle non-finite values.
Results may differ from a plain program's by a relative error of at most 0.00002.
Values sent between devices are 32-bit elements; how exact they have to be, the bound alone decides.
A program may use at most 64 MiB of HBM per device.

v0:
```python
import math

import jax
import jax.numpy as jnp
from jax import lax
from jax.sharding import PartitionSpec as P

B = 256


def broadcast(value, axis, source):
    kept = jnp.where(lax.axis_index(axis) == source, value, 0).astype(value.dtype)
    return lax.psum(kept, axis)


def tropical_product(left_panel, right_panel, accumulated):
    height, inner_width = left_panel.shape
    breadth = right_panel.shape[1]
    piece_width = math.gcd(32, inner_width)
    piece_count = inner_width // piece_width
    left_pieces = left_panel.reshape(height, piece_count, piece_width).transpose(1, 0, 2)
    right_pieces = right_panel.reshape(piece_count, piece_width, breadth)

    def fold_piece(running, operands):
        left_piece, right_piece = operands
        sums = left_piece[:, :, None] + right_piece[None, :, :]
        return (jnp.minimum(running, jnp.min(sums, axis=1)), None)

    result, unused = lax.scan(fold_piece, accumulated, (left_pieces, right_pieces))
    return result


def close_sequential(pivot_block):

    def relax(column_index, current):
        through_col = lax.dynamic_slice_in_dim(current, column_index, 1, 1)
        through_row = lax.dynamic_slice_in_dim(current, column_index, 1, 0)
        return jnp.minimum(current, through_col + through_row)

    return lax.fori_loop(0, pivot_block.shape[0], relax, pivot_block)


def on_device(distances):
    tile_rows, tile_cols = distances.shape
    col_count = lax.axis_size("col")
    my_row = lax.axis_index("row")
    my_col = lax.axis_index("col")
    current = distances
    row_owner = 0 // tile_rows
    col_owner = 0 // tile_cols
    row_offset = 0 % tile_rows
    col_offset = 0 % tile_cols
    corner = current[row_offset : row_offset + B, col_offset : col_offset + B]
    pivot = broadcast(corner, ("row", "col"), row_owner * col_count + col_owner)
    closed = close_sequential(pivot)
    row_strip = current[row_offset : row_offset + B, :]
    col_strip = current[:, col_offset : col_offset + B]

    def update_rows(strip):
        return tropical_product(closed, strip, strip)

    def update_cols(strip):
        return tropical_product(strip, closed, strip)

    def unchanged(strip):
        return strip

    row_strip = lax.cond(my_row == row_owner, update_rows, unchanged, row_strip)
    col_strip = lax.cond(my_col == col_owner, update_cols, unchanged, col_strip)
    row_panel = broadcast(row_strip, "row", row_owner)
    col_panel = broadcast(col_strip, "col", col_owner)
    current = tropical_product(col_panel, row_panel, current)
    return current


def solution(mesh):
    in_specs = (P("row", "col"),)
    out_specs = P("row", "col")
    return jax.shard_map(
        on_device, mesh=mesh, in_specs=in_specs, out_specs=out_specs, check_vma=False
    )
```

profile of v0, /device:TPU:61, one launch (start us, length us, event | category | flops | bytes accessed | tf_op | source)
XLA Modules:
  0.0 2143.3 jit_solution(4921819519769510484)
XLA Ops:
  10.4 255.5 %all-reduce.4.cloned.1.call-done = f32[256,256]{1,0:T(8,128)} async-done(((f32[256,256]{1,0:T(8,128)}), f32[256,256]{1,0:T(8,128)}) %all-reduce.4.cloned.1.call-update) | async-done | bytes 262160 | tf_op jit(solution)/shard_map/psum | solution.py:13
  266.0 907.7 %while.43 = (s32[]{:T(128)}, f32[256,256]{1,0:T(8,128)}, s32[]{:T(128)}) while((s32[]{:T(128)}, f32[256,256]{1,0:T(8,128)}, s32[]{:T(128)}) %tuple.100), condition=%wide.region_2.3_spmd, body=%wide.region_1.2_spmd.sunk | while | flops 131074 | bytes 530485 | solution.py:40
  267.7 1.8 add_minimum_fusion.2
  271.3 1.8 add_minimum_fusion.2
  274.8 1.8 add_minimum_fusion.2
  278.4 1.8 add_minimum_fusion.2
  281.9 1.8 add_minimum_fusion.2
  285.5 1.8 add_minimum_fusion.2
  292.6 1.8 add_minimum_fusion.2
  299.7 1.8 add_minimum_fusion.2
  306.8 1.8 add_minimum_fusion.2
  313.8 1.8 add_minimum_fusion.2
  320.9 1.8 add_minimum_fusion.2
  328.0 1.8 add_minimum_fusion.2
  335.1 1.8 add_minimum_fusion.2
  338.7 1.8 add_minimum_fusion.2
  342.2 1.8 add_minimum_fusion.2
  345.8 1.8 add_minimum_fusion.2
  349.3 1.8 add_minimum_fusion.2
  352.8 1.8 add_minimum_fusion.2
  359.9 1.8 add_minimum_fusion.2
  367.0 1.8 add_minimum_fusion.2
  374.1 1.8 add_minimum_fusion.2
  381.2 1.8 add_minimum_fusion.2
  388.3 1.8 add_minimum_fusion.2
  395.4 1.8 add_minimum_fusion.2
  402.5 1.8 add_minimum_fusion.2
  406.0 1.8 add_minimum_fusion.2
  409.6 1.8 add_minimum_fusion.2
  413.1 1.8 add_minimum_fusion.2
  416.7 1.8 add_minimum_fusion.2
  420.2 1.8 add_minimum_fusion.2
  427.3 1.8 add_minimum_fusion.2
  434.4 1.8 add_minimum_fusion.2
  441.5 1.8 add_minimum_fusion.2
  448.6 1.8 add_minimum_fusion.2
  455.7 1.8 add_minimum_fusion.2
  462.8 1.8 add_minimum_fusion.2
  469.9 1.8 add_minimum_fusion.2
  473.4 1.8 add_minimum_fusion.2
  477.0 1.8 add_minimum_fusion.2
  480.5 1.8 add_minimum_fusion.2
  484.0 1.8 add_minimum_fusion.2
  487.6 1.8 add_minimum_fusion.2
  494.7 1.8 add_minimum_fusion.2
  501.8 1.8 add_minimum_fusion.2
  508.9 1.8 add_minimum_fusion.2
  516.0 1.8 add_minimum_fusion.2
  523.0 1.8 add_minimum_fusion.2
  530.1 1.8 add_minimum_fusion.2
  537.2 1.8 add_minimum_fusion.2
  540.8 1.8 add_minimum_fusion.2
  544.3 1.8 add_minimum_fusion.2
  1175.9 92.5 %all-reduce.6.cloned.1.call-done = f32[8,384,32]{1,2,0:T(8,128)} async-done(((f32[8,384,32]{1,2,0:T(8,128)}), f32[8,384,32]{1,2,0:T(8,128)}) %all-reduce.6.cloned.1.call-update) | async-done | bytes 393232 | tf_op jit(solution)/shard_map/psum | solution.py:13
  1268.4 487.7 %all-reduce.8.cloned.1.call-done = f32[8,32,1536]{2,1,0:T(8,128)} async-done(((f32[8,32,1536]{2,1,0:T(8,128)}), f32[8,32,1536]{2,1,0:T(8,128)}) %all-reduce.8.cloned.1.call-update) | async-done | bytes 1572880 | tf_op jit(solution)/shard_map/psum | solution.py:13
  1756.0 379.4 %while.44 = (s32[]{:T(128)}, f32[384,1536]{1,0:T(8,128)S(1)}, f32[8,384,32]{1,2,0:T(8,128)}, f32[8,32,1536]{2,1,0:T(8,128)}, s32[]{:T(128)}) while((s32[]{:T(128)}, f32[384,1536]{1,0:T(8,128)S(1)}, f32[8,384,32]{1,2,0:T(8,128)}, f32[8,32,1536]{2,1,0:T(8,128)}, s32[]{:T(128)}) %tuple.105), condition=%wide.region_17.18_spmd, body=%wide.region_15.17_spmd.sunk | while | flops 37748736 | bytes 10272837 | solution.py:29
  1757.9 44.9 %add_reduce_fusion.6 = f32[384,1536]{1,0:T(8,128)S(1)} fusion(f32[32,1536]{1,0:T(8,128)S(1)} %dynamic-slice_bitcast_fusion.6, f32[384,32]{1,0:T(8,128)S(1)} %bitcast.39), kind=kLoop, calls=%fused_computation.6.clone.1 | loop fusion | flops 37158912 | bytes 2605056 | tf_op jit(solution)/shard_map/while/body/eval_jaxpr/reduce_min | solution.py:27
  1805.3 44.9 %add_reduce_fusion.6 = f32[384,1536]{1,0:T(8,128)S(1)} fusion(f32[32,1536]{1,0:T(8,128)S(1)} %dynamic-slice_bitcast_fusion.6, f32[384,32]{1,0:T(8,128)S(1)} %bitcast.39), kind=kLoop, calls=%fused_computation.6.clone.1 | loop fusion | flops 37158912 | bytes 2605056 | tf_op jit(solution)/shard_map/while/body/eval_jaxpr/reduce_min | solution.py:27
  1852.8 44.9 %add_reduce_fusion.6 = f32[384,1536]{1,0:T(8,128)S(1)} fusion(f32[32,1536]{1,0:T(8,128)S(1)} %dynamic-slice_bitcast_fusion.6, f32[384,32]{1,0:T(8,128)S(1)} %bitcast.39), kind=kLoop, calls=%fused_computation.6.clone.1 | loop fusion | flops 37158912 | bytes 2605056 | tf_op jit(solution)/shard_map/while/body/eval_jaxpr/reduce_min | solution.py:27
  1900.2 44.9 %add_reduce_fusion.6 = f32[384,1536]{1,0:T(8,128)S(1)} fusion(f32[32,1536]{1,0:T(8,128)S(1)} %dynamic-slice_bitcast_fusion.6, f32[384,32]{1,0:T(8,128)S(1)} %bitcast.39), kind=kLoop, calls=%fused_computation.6.clone.1 | loop fusion | flops 37158912 | bytes 2605056 | tf_op jit(solution)/shard_map/while/body/eval_jaxpr/reduce_min | solution.py:27
  1947.6 44.9 %add_reduce_fusion.6 = f32[384,1536]{1,0:T(8,128)S(1)} fusion(f32[32,1536]{1,0:T(8,128)S(1)} %dynamic-slice_bitcast_fusion.6, f32[384,32]{1,0:T(8,128)S(1)} %bitcast.39), kind=kLoop, calls=%fused_computation.6.clone.1 | loop fusion | flops 37158912 | bytes 2605056 | tf_op jit(solution)/shard_map/while/body/eval_jaxpr/reduce_min | solution.py:27
  1995.0 44.9 %add_reduce_fusion.6 = f32[384,1536]{1,0:T(8,128)S(1)} fusion(f32[32,1536]{1,0:T(8,128)S(1)} %dynamic-slice_bitcast_fusion.6, f32[384,32]{1,0:T(8,128)S(1)} %bitcast.39), kind=kLoop, calls=%fused_computation.6.clone.1 | loop fusion | flops 37158912 | bytes 2605056 | tf_op jit(solution)/shard_map/while/body/eval_jaxpr/reduce_min | solution.py:27
  2042.5 44.9 %add_reduce_fusion.6 = f32[384,1536]{1,0:T(8,128)S(1)} fusion(f32[32,1536]{1,0:T(8,128)S(1)} %dynamic-slice_bitcast_fusion.6, f32[384,32]{1,0:T(8,128)S(1)} %bitcast.39), kind=kLoop, calls=%fused_computation.6.clone.1 | loop fusion | flops 37158912 | bytes 2605056 | tf_op jit(solution)/shard_map/while/body/eval_jaxpr/reduce_min | solution.py:27
  2089.9 44.9 %add_reduce_fusion.6 = f32[384,1536]{1,0:T(8,128)S(1)} fusion(f32[32,1536]{1,0:T(8,128)S(1)} %dynamic-slice_bitcast_fusion.6, f32[384,32]{1,0:T(8,128)S(1)} %bitcast.39), kind=kLoop, calls=%fused_computation.6.clone.1 | loop fusion | flops 37158912 | bytes 2605056 | tf_op jit(solution)/shard_map/while/body/eval_jaxpr/reduce_min | solution.py:27
  (766 shorter events, 844.0 us)
Async XLA Ops:
  6.5 259.4 %all-reduce.4.cloned.1.call-start = ((), (), s32[]{:S(2)}) async-start(), calls=%async_computation | async-start | bytes 524288 | tf_op jit(solution)/shard_map/psum | solution.py:13
  8.9 1259.4 %all-reduce.6.cloned.1.call-start = ((), (), s32[]{:S(2)}) async-start(), calls=%async_computation.1 | async-start | bytes 786432 | tf_op jit(solution)/shard_map/psum | solution.py:13
  1174.5 581.5 %all-reduce.8.cloned.1.call-start = ((), (), s32[]{:S(2)}) async-start(), calls=%async_computation.2 | async-start | bytes 3145728 | tf_op jit(solution)/shard_map/psum | solution.py:13
  2135.4 1.4 copy-start
Sparse Core Ops, SparseCore 0:
  12.8 253.1 all-reduce.3
  1174.6 93.6 all-reduce.5
  1271.6 484.3 all-reduce.7
where the time goes:
time: 2170 us; the launch traced here: 2140 us
  waiting for transfers between devices  836 us (39%)
  other arithmetic  818 us (38%)
  local copies, waits for them, and re-layouts  475 us (22%)
    psum x3, waiting for transfers between devices, broadcast(): return lax.psum(kept, axis)  836 us
    min x256, other arithmetic, relax(): return jnp.minimum(current, through_col + through_row)  451 us
    reduce_min x8, other arithmetic, fold_piece(): return (jnp.minimum(running, jnp.min(sums, axis=1)), None)  359 us
    dynamic_slice x256, local copies, waits for them, and re-layouts, relax(): through_col = lax.dynamic_slice_in_dim(current, column_index, 1, 1)  276 us
    dynamic_slice x256, local copies, waits for them, and re-layouts, relax(): through_row = lax.dynamic_slice_in_dim(current, column_index, 1, 0)  179 us
  transfers between devices with their start and end apart: 3, of which 3 were waited for; matrix products, arithmetic and copies ran while one was open for 0% of the time, Pallas kernels for 0%

commit v1 on v0

v1 whole, which is shorter than its diff:
```python
import functools

import jax
import jax.numpy as jnp
from jax import lax
from jax.experimental import pallas as pl
from jax.experimental.pallas import tpu as pltpu
from jax.sharding import PartitionSpec as P

B = 256
NB = 32
MESH = pl.DeviceIdType.MESH
STEP = ((1, 0), (0, 1), (3, 0), (0, 3))
SENDS = ((0, 4, 5, 6, 8, 9, 10, 11), (4, 5), (5, 6, 7), (4, 8))


def member(value, items):
    return functools.reduce(jnp.logical_or, [value == i for i in items])


def gather_kernel(d_ref, c_ref, r_ref, p_ref, csend, crecv, rsend, rrecv, psend, precv):
    row, z = lax.axis_index("row"), lax.axis_index("col")
    core, chip = row % 2, row // 2
    x, y = chip % 4, chip // 4
    sibling = (row + 1 - 2 * core, z)
    root = chip == 0
    plus = z < 4
    minus = jnp.logical_or(z == 0, z > 5)
    up, down = (row, (z + 1) % 8), (row, (z + 7) % 8)

    def chip_at(dx, dy):
        return (2 * (((y + dy) % 4) * 4 + (x + dx) % 4) + core, z)

    def number(flag):
        return jnp.where(flag, 1, 0)

    frame = ((x, y), (y, (4 - x) % 4), ((4 - x) % 4, (4 - y) % 4), ((4 - y) % 4, x))
    forks = []
    for q in range(4):
        place = frame[q][0] * 4 + frame[q][1]
        forks.append([(member(place, SENDS[d]), chip_at(*STEP[(d + q) % 4])) for d in range(4)])

    barrier = pltpu.get_barrier_semaphore()

    def greet(device):
        pl.semaphore_signal(barrier, inc=1, device_id=device, device_id_type=MESH)

    greet(sibling)

    @pl.when(jnp.logical_and(z > 0, z < 5))
    def _():
        greet(down)

    @pl.when(z > 4)
    def _():
        greet(up)

    @pl.when(chip > 0)
    def _():
        for d in range(4):
            greet(chip_at(*STEP[d]))

    beside_root = member(chip, (1, 3, 4, 12))
    pl.semaphore_wait(barrier, 5 + number(plus) + number(minus) - number(beside_root))

    def remote(src, dst, send_sem, recv_sem, device):
        return pltpu.make_async_remote_copy(
            src_ref=src, dst_ref=dst, send_sem=send_sem, recv_sem=recv_sem, device_id=device, device_id_type=MESH
        )

    def start(flag, copy):
        @pl.when(flag)
        def _():
            copy.start()

    def finish(flag, part, send_sem, recv_sem):
        @pl.when(flag)
        def _():
            remote(part, part, send_sem, recv_sem, sibling).wait_send()

    nc = c_ref.shape[0] // NB
    width = r_ref.shape[1] // 4

    def c_part(i):
        return pl.ds(i * NB, NB), slice(0, B)

    def r_part(q, j):
        return pl.ds(j * NB, NB), slice(q * width, (q + 1) * width)

    @pl.when(z == 0)
    def _():
        for i in range(nc):
            part = c_ref.at[c_part(i)]
            pltpu.make_async_copy(d_ref.at[c_part(i)], part, crecv.at[i]).start()

    root0 = jnp.logical_and(root, core == 0)
    for j in range(B // NB):
        for q in range(4):
            part = r_part(q, j)

            @pl.when(root0)
            def _():
                pltpu.make_async_copy(d_ref.at[part], r_ref.at[part], rrecv.at[q, j]).start()

            start(root0, remote(d_ref.at[part], r_ref.at[part], rsend.at[q, j, 4], rrecv.at[q, j], sibling))

    def take_c(i):
        part = c_ref.at[c_part(i)]
        remote(part, part, csend.at[i, 0], crecv.at[i], up).wait_recv()
        start(plus, remote(part, part, csend.at[i, 0], crecv.at[i], up))
        start(minus, remote(part, part, csend.at[i, 1], crecv.at[i], down))
        if i < B // NB:

            @pl.when(root0)
            def _():
                pltpu.make_async_copy(part, p_ref.at[c_part(i)], precv.at[i]).start()

    def take_r(q, j):
        part = r_ref.at[r_part(q, j)]
        remote(part, part, rsend.at[q, j, 0], rrecv.at[q, j], sibling).wait_recv()
        for d, (flag, device) in enumerate(forks[q]):
            start(jnp.logical_and(core == 1, flag), remote(part, part, rsend.at[q, j, d], rrecv.at[q, j], device))
        start(
            jnp.logical_and(core == 1, chip > 0),
            remote(part, part, rsend.at[q, j, 4], rrecv.at[q, j], sibling),
        )

    def take_p(i):
        part = p_ref.at[c_part(i)]
        remote(part, part, psend.at[i, 0], precv.at[i], sibling).wait_recv()
        for d, (flag, device) in enumerate(forks[i % 4]):
            start(jnp.logical_and(core == 0, flag), remote(part, part, psend.at[i, d], precv.at[i], device))
        start(core == 0, remote(part, part, psend.at[i, 4], precv.at[i], sibling))

    n = B // NB

    @pl.when(core == 0)
    def _():
        for i in range(n):
            take_c(i)
        for i in range(n):
            take_p(i)
            if i % 2 == 1:
                take_c(n + i // 2)
        for j in range(n):
            for q in range(4):
                take_r(q, j)

    @pl.when(core == 1)
    def _():
        for j in range(n):
            for q in range(4):
                take_r(q, j)
            take_c(j)
        for i in range(n, nc):
            take_c(i)
        for i in range(n):
            take_p(i)

    for i in range(nc):
        part = c_ref.at[c_part(i)]
        finish(plus, part, csend.at[i, 0], crecv.at[i])
        finish(minus, part, csend.at[i, 1], crecv.at[i])
    for j in range(n):
        for q in range(4):
            part = r_ref.at[r_part(q, j)]
            for d in range(4):
                finish(jnp.logical_and(core == 1, forks[q][d][0]), part, rsend.at[q, j, d], rrecv.at[q, j])
            own = jnp.logical_or(root0, jnp.logical_and(core == 1, chip > 0))
            finish(own, part, rsend.at[q, j, 4], rrecv.at[q, j])
    for i in range(n):
        part = p_ref.at[c_part(i)]
        for d in range(4):
            finish(jnp.logical_and(core == 0, forks[i % 4][d][0]), part, psend.at[i, d], precv.at[i])
        finish(core == 0, part, psend.at[i, 4], precv.at[i])


def gather(distances):
    rows, cols = distances.shape
    f32 = jnp.float32
    return pl.pallas_call(
        gather_kernel,
        out_shape=(
            jax.ShapeDtypeStruct((rows, B), f32),
            jax.ShapeDtypeStruct((B, cols), f32),
            jax.ShapeDtypeStruct((B, B), f32),
        ),
        in_specs=[pl.BlockSpec(memory_space=pl.ANY)],
        out_specs=[pl.BlockSpec(memory_space=pltpu.VMEM)] * 3,
        scratch_shapes=[
            pltpu.SemaphoreType.DMA((rows // NB, 2)),
            pltpu.SemaphoreType.DMA((rows // NB,)),
            pltpu.SemaphoreType.DMA((4, B // NB, 5)),
            pltpu.SemaphoreType.DMA((4, B // NB)),
            pltpu.SemaphoreType.DMA((B // NB, 5)),
            pltpu.SemaphoreType.DMA((B // NB,)),
        ],
        compiler_params=pltpu.CompilerParams(collective_id=0, has_side_effects=True),
        name="gather",
    )(distances)


def panel_update(x_ref, row0, rows, panel_ref, k, group):
    def step(g, carry):
        part = pl.ds(pl.multiple_of(row0 + g * group, 8), group)
        value = x_ref[part, :]
        left = x_ref[part, k : k + NB]
        for l in range(NB):
            value = jnp.minimum(value, left[:, l : l + 1] + panel_ref[k + l : k + l + 1, :])
        x_ref[part, :] = value
        return carry

    lax.fori_loop(0, rows // group, step, 0)


def close_and_extend(pivot_ref, panel_ref, x_ref):
    for k in range(0, B, NB):
        here = k // 128 * 128
        other = 128 - here
        rows = pl.ds(k, NB)
        square = pivot_ref[rows, here : here + 128]
        panel_ref[rows, here : here + 128] = square
        for _ in range(5):
            left = square[:, k - here : k - here + NB]
            for l in range(NB):
                square = jnp.minimum(square, left[:, l : l + 1] + panel_ref[k + l : k + l + 1, here : here + 128])
            panel_ref[rows, here : here + 128] = square
        left = square[:, k - here : k - here + NB]
        value = pivot_ref[rows, other : other + 128]
        for l in range(NB):
            value = jnp.minimum(value, left[:, l : l + 1] + pivot_ref[k + l : k + l + 1, other : other + 128])
        panel_ref[rows, other : other + 128] = value
        if k + NB < B:
            panel_update(pivot_ref, k + NB, B - k - NB, panel_ref, k, 32)
        panel_update(x_ref, 0, x_ref.shape[0], panel_ref, k, 64)


TI, TJ, U = 24, 512, 32


def min_plus(x_ref, y_ref, acc_ref, out_ref, wide_ref):
    height, depth = x_ref.shape
    breadth = y_ref.shape[1]
    blocks, strips = height // TI, breadth // TJ
    share = 8 * (-(-(TI // 8) // strips))

    def widen(slot, left, row0, l0):
        for u in range(U):
            wide_ref[slot, l0 + u, row0 : row0 + share, :] = jnp.broadcast_to(left[:, u : u + 1], (share, 128))
        return pltpu.roll(left, 128 - U, 1)

    for s in range(TI // share):
        for half in range(depth // 128):

            def first(g, left):
                return widen(0, left, s * share, pl.multiple_of(half * 128 + g * U, U))

            lax.fori_loop(0, 128 // U, first, x_ref[s * share : (s + 1) * share, half * 128 : half * 128 + 128])

    def block(b, carry):
        slot = lax.rem(b, 2)
        row0 = pl.multiple_of(b * TI, TI)
        next0 = pl.multiple_of(jnp.minimum(b + 1, blocks - 1) * TI, TI)
        for s in range(strips):
            strip = slice(s * TJ, (s + 1) * TJ)
            value = acc_ref[pl.ds(row0, TI), strip]
            for half in range(depth // 128):

                def group(g, state):
                    value, left = state
                    l0 = pl.multiple_of(half * 128 + g * U, U)
                    right = y_ref.at[pl.ds(l0, U), strip]
                    for u in range(U):
                        wide = wide_ref[slot, l0 + u]
                        row = right[pl.ds(u, 8, stride=0), :]
                        value = jnp.concatenate(
                            [
                                jnp.minimum(
                                    value[:, c : c + 128], wide + jnp.concatenate([row[:, c : c + 128]] * (TI // 8), 0)
                                )
                                for c in range(0, TJ, 128)
                            ],
                            1,
                        )
                    if s * share < TI:
                        left = widen(1 - slot, left, s * share, l0)
                    return value, left

                left = x_ref[pl.ds(next0 + s * share, share), half * 128 : half * 128 + 128]
                value, left = lax.fori_loop(0, 128 // U, group, (value, left))
            out_ref[pl.ds(row0, TI), strip] = value
        return carry

    lax.fori_loop(0, blocks, block, 0)


def update_kernel(c_ref, r_ref, p_ref, d_ref, out_ref, x_ref, pivot_ref, panel_ref, wide_ref):
    pivot_ref[...] = p_ref[...]
    x_ref[...] = c_ref[...]
    close_and_extend(pivot_ref, panel_ref, x_ref)
    min_plus(x_ref, r_ref, d_ref, out_ref, wide_ref)


def on_device(distances):
    rows, cols = distances.shape
    f32 = jnp.float32
    c, r, p = gather(distances)
    return pl.pallas_call(
        update_kernel,
        out_shape=jax.ShapeDtypeStruct((rows, cols), f32),
        in_specs=[pl.BlockSpec(memory_space=pltpu.VMEM)] * 4,
        out_specs=pl.BlockSpec(memory_space=pltpu.VMEM),
        scratch_shapes=[
            pltpu.VMEM((rows, B), f32),
            pltpu.VMEM((B, B), f32),
            pltpu.VMEM((B, B), f32),
            pltpu.VMEM((2, B, TI, 128), f32),
        ],
        name="update",
    )(c, r, p, distances)


def solution(mesh):
    spec = P("row", "col")
    return jax.shard_map(on_device, mesh=mesh, in_specs=(spec,), out_specs=spec, check_vma=False)
```

time: 2170 us -> 278 us (0.13)
  the two profiles are of different devices: /device:TPU:61 before, /device:TPU:141 now
where the time goes in v1:
time: 278 us; the launch traced here: 277 us
  Pallas kernels  277 us (100%)
    pallas_call x1, Pallas kernels, gather(): pl.pallas_call(gather_kernel, out_shape=(jax.ShapeDtypeStruct((rows, B),...  183 us
    pallas_call x1, Pallas kernels, on_device(): pl.pallas_call(update_kernel, out_shape=jax.ShapeDtypeStruct((rows, cols)...  93.9 us

profile of v1, /device:TPU:141, one launch (start us, length us, event | category | flops | bytes accessed | tf_op | source)
XLA Modules:
  0.0 277.4 jit_solution(2934172793589609141)
XLA Ops:
  0.0 183.5 %gather.1 = (f32[384,256]{1,0:T(8,128)}, f32[256,1536]{1,0:T(8,128)}, f32[256,256]{1,0:T(8,128)}) custom-call(f32[384,1536]{1,0:T(8,128)} %d_ref.3), custom_call_target="tpu_custom_call" | custom-call | tf_op jit(solution)/shard_map/gather/pallas_call | solution.py:181
  183.5 93.9 %update.1 = f32[384,1536]{1,0:T(8,128)} custom-call(f32[384,256]{1,0:T(8,128)} %get-tuple-element.8.c_ref, f32[256,1536]{1,0:T(8,128)} %get-tuple-element.9.r_ref, f32[256,256]{1,0:T(8,128)} %get-tuple-element.10.p_ref, f32[384,1536]{1,0:T(8,128)} %d_ref.3), custom_call_target="tpu_custom_call" | custom-call | tf_op jit(solution)/shard_map/update/pallas_call | solution.py:308

commit v2 on v1

--- a/solution.py
+++ b/solution.py
@@ -12,6 +12,8 @@
 MESH = pl.DeviceIdType.MESH
 STEP = ((1, 0), (0, 1), (3, 0), (0, 3))
 SENDS = ((0, 4, 5, 6, 8, 9, 10, 11), (4, 5), (5, 6, 7), (4, 8))
+DEPTHS = ((0,), (4,), (5, 7, 8), (1, 6, 9, 3, 11, 12), (2, 10, 13, 15), (14,))
+HOP = 4
 
 
 def member(value, items):
@@ -82,10 +84,10 @@
     width = r_ref.shape[1] // 4
 
     def c_part(i):
-        return pl.ds(i * NB, NB), slice(0, B)
+        return pl.ds(pl.multiple_of(i * NB, NB), NB), slice(0, B)
 
     def r_part(q, j):
-        return pl.ds(j * NB, NB), slice(q * width, (q + 1) * width)
+        return pl.ds(pl.multiple_of(j * NB, NB), NB), slice(q * width, (q + 1) * width)
 
     @pl.when(z == 0)
     def _():
@@ -94,80 +96,103 @@
             pltpu.make_async_copy(d_ref.at[c_part(i)], part, crecv.at[i]).start()
 
     root0 = jnp.logical_and(root, core == 0)
-    for j in range(B // NB):
-        for q in range(4):
-            part = r_part(q, j)
-
-            @pl.when(root0)
-            def _():
+
+    @pl.when(root0)
+    def _():
+        @pl.loop(0, B // NB)
+        def _(j):
+            for q in range(4):
+                part = r_part(q, j)
                 pltpu.make_async_copy(d_ref.at[part], r_ref.at[part], rrecv.at[q, j]).start()
-
-            start(root0, remote(d_ref.at[part], r_ref.at[part], rsend.at[q, j, 4], rrecv.at[q, j], sibling))
+                remote(d_ref.at[part], r_ref.at[part], rsend.at[q, j, 4], rrecv.at[q, j], sibling).start()
+
+    n = B // NB
+    reach = jnp.where(z < 5, z, 8 - z)
+    depth = []
+    for q in range(4):
+        place = frame[q][0] * 4 + frame[q][1]
+        depth.append(sum(number(member(place, DEPTHS[k])) * k for k in range(1, 6)))
 
     def take_c(i):
         part = c_ref.at[c_part(i)]
         remote(part, part, csend.at[i, 0], crecv.at[i], up).wait_recv()
         start(plus, remote(part, part, csend.at[i, 0], crecv.at[i], up))
         start(minus, remote(part, part, csend.at[i, 1], crecv.at[i], down))
-        if i < B // NB:
-
-            @pl.when(root0)
-            def _():
-                pltpu.make_async_copy(part, p_ref.at[c_part(i)], precv.at[i]).start()
+
+        @pl.when(jnp.logical_and(root0, i < n))
+        def _():
+            pltpu.make_async_copy(part, p_ref.at[c_part(i)], precv.at[i]).start()
 
     def take_r(q, j):
         part = r_ref.at[r_part(q, j)]
         remote(part, part, rsend.at[q, j, 0], rrecv.at[q, j], sibling).wait_recv()
         for d, (flag, device) in enumerate(forks[q]):
-            start(jnp.logical_and(core == 1, flag), remote(part, part, rsend.at[q, j, d], rrecv.at[q, j], device))
-        start(
-            jnp.logical_and(core == 1, chip > 0),
-            remote(part, part, rsend.at[q, j, 4], rrecv.at[q, j], sibling),
-        )
+            start(flag, remote(part, part, rsend.at[q, j, d], rrecv.at[q, j], device))
+        start(chip > 0, remote(part, part, rsend.at[q, j, 4], rrecv.at[q, j], sibling))
 
     def take_p(i):
         part = p_ref.at[c_part(i)]
         remote(part, part, psend.at[i, 0], precv.at[i], sibling).wait_recv()
         for d, (flag, device) in enumerate(forks[i % 4]):
-            start(jnp.logical_and(core == 0, flag), remote(part, part, psend.at[i, d], precv.at[i], device))
-        start(core == 0, remote(part, part, psend.at[i, 4], precv.at[i], sibling))
-
-    n = B // NB
+            start(flag, remote(part, part, psend.at[i, d], precv.at[i], device))
+        start(True, remote(part, part, psend.at[i, 4], precv.at[i], sibling))
+
+    @pl.loop(0, 5 * HOP + 4 * HOP + 3 * nc // 2 + 2)
+    def _(t):
+        u = t - HOP * reach
+        i = (2 * u + u % 3) // 3
+
+        @pl.when(jnp.logical_and(jnp.logical_and(u >= 0, u % 3 < 2), i < nc))
+        def _():
+            take_c(i)
+
+        @pl.when(core == 0)
+        def _():
+            for i in range(n):
+
+                @pl.when(u == 3 * i // 2 + 1 + HOP * depth[i % 4])
+                def _():
+                    take_p(i)
+
+        @pl.when(core == 1)
+        def _():
+            for q in range(4):
+                j = t - HOP * depth[q]
+
+                @pl.when(jnp.logical_and(j >= 0, j < n))
+                def _():
+                    take_r(q, j)
 
     @pl.when(core == 0)
     def _():
-        for i in range(n):
-            take_c(i)
-        for i in range(n):
-            take_p(i)
-            if i % 2 == 1:
-                take_c(n + i // 2)
-        for j in range(n):
+        @pl.loop(0, n)
+        def _(j):
             for q in range(4):
-                take_r(q, j)
+                part = r_ref.at[r_part(q, j)]
+                remote(part, part, rsend.at[q, j, 0], rrecv.at[q, j], sibling).wait_recv()
 
     @pl.when(core == 1)
     def _():
-        for j in range(n):
-            for q in range(4):
-                take_r(q, j)
-            take_c(j)
-        for i in range(n, nc):
-            take_c(i)
-        for i in range(n):
-            take_p(i)
-
-    for i in range(nc):
+        @pl.loop(0, n)
+        def _(i):
+            part = p_ref.at[c_part(i)]
+            remote(part, part, psend.at[i, 0], precv.at[i], sibling).wait_recv()
+
+    @pl.loop(0, nc)
+    def _(i):
         part = c_ref.at[c_part(i)]
         finish(plus, part, csend.at[i, 0], crecv.at[i])
         finish(minus, part, csend.at[i, 1], crecv.at[i])
-    for j in range(n):
+
+    @pl.loop(0, n)
+    def _(j):
         for q in range(4):
             part = r_ref.at[r_part(q, j)]
             for d in range(4):
                 finish(jnp.logical_and(core == 1, forks[q][d][0]), part, rsend.at[q, j, d], rrecv.at[q, j])
             own = jnp.logical_or(root0, jnp.logical_and(core == 1, chip > 0))
             finish(own, part, rsend.at[q, j, 4], rrecv.at[q, j])
+
     for i in range(n):
         part = p_ref.at[c_part(i)]
         for d in range(4):

time: 278 us -> 137 us (0.49)
  Pallas kernels: 277 us -> 137 us
    pallas_call x1, Pallas kernels: 183 us -> 42.8 us  [gather(): pl.pallas_call(gather_kernel, out_shape=(jax.ShapeDtypeStruct((rows, B),...]
where the time goes in v2:
time: 137 us
  Pallas kernels  137 us (100%)
    pallas_call x1, Pallas kernels, on_device(): pl.pallas_call(update_kernel, out_shape=jax.ShapeDtypeStruct((rows, cols)...  93.9 us
    pallas_call x1, Pallas kernels, gather(): pl.pallas_call(gather_kernel, out_shape=(jax.ShapeDtypeStruct((rows, B),...  42.8 us

profile of v2, /device:TPU:141, one launch (start us, length us, event | category | flops | bytes accessed | tf_op | source)
XLA Modules:
  0.0 136.7 jit_solution(3081410423349528591)
XLA Ops:
  0.0 42.8 %gather.1 = (f32[384,256]{1,0:T(8,128)}, f32[256,1536]{1,0:T(8,128)}, f32[256,256]{1,0:T(8,128)}) custom-call(f32[384,1536]{1,0:T(8,128)} %d_ref.3), custom_call_target="tpu_custom_call" | custom-call | tf_op jit(solution)/shard_map/gather/pallas_call | solution.py:206
  42.8 93.9 %update.1 = f32[384,1536]{1,0:T(8,128)} custom-call(f32[384,256]{1,0:T(8,128)} %get-tuple-element.8.c_ref, f32[256,1536]{1,0:T(8,128)} %get-tuple-element.9.r_ref, f32[256,256]{1,0:T(8,128)} %get-tuple-element.10.p_ref, f32[384,1536]{1,0:T(8,128)} %d_ref.3), custom_call_target="tpu_custom_call" | custom-call | tf_op jit(solution)/shard_map/update/pallas_call | solution.py:333

commit v3 on v2

v3 whole, which is shorter than its diff:
```python
import functools

import jax
import jax.numpy as jnp
from jax import lax
from jax.experimental import pallas as pl
from jax.experimental.pallas import tpu as pltpu
from jax.sharding import PartitionSpec as P

B = 256
NB = 32
KB = 16
MESH = pl.DeviceIdType.MESH
STEP = ((1, 0), (0, 1), (3, 0), (0, 3))
SENDS = ((0, 4, 5, 6, 8, 9, 10, 11), (4, 5), (5, 6, 7), (4, 8))
DEPTHS = ((0,), (4,), (5, 7, 8), (1, 6, 9, 3, 11, 12), (2, 10, 13, 15), (14,))
TAKES = ((4, 8, 9, 10, 12, 13, 14, 15), (5, 6), (1, 2, 3), (7, 11))
HOP = 4


def member(value, items):
    return functools.reduce(jnp.logical_or, [value == i for i in items])


def gather_kernel(d_ref, c_ref, r_ref, p_ref, csend, crecv, rsend, rrecv, psend, precv):
    row, z = lax.axis_index("row"), lax.axis_index("col")
    core, chip = row % 2, row // 2
    x, y = chip % 4, chip // 4
    sibling = (row + 1 - 2 * core, z)
    root = row == 0
    plus = z < 4
    minus = jnp.logical_or(z == 0, z > 5)
    up, down = (row, (z + 1) % 8), (row, (z + 7) % 8)
    n, nc = B // NB, c_ref.shape[0] // NB
    width = r_ref.shape[1] // 4

    def number(flag):
        return jnp.where(flag, 1, 0)

    def both(*flags):
        return functools.reduce(jnp.logical_and, flags)

    def chip_at(step, side):
        dx, dy = step
        return (2 * (((y + dy) % 4) * 4 + (x + dx) % 4) + side, z)

    frame = ((x, y), (y, (4 - x) % 4), ((4 - x) % 4, (4 - y) % 4), ((4 - y) % 4, x))
    forks, depth, mine = [], [], []
    barrier = pltpu.get_barrier_semaphore()

    def greet(device):
        pl.semaphore_signal(barrier, inc=1, device_id=device, device_id_type=MESH)

    expected = 1 + number(plus) + number(minus)
    for q in range(4):
        side = q // 2
        place = frame[q][0] * 4 + frame[q][1]
        mine.append(both(chip > 0, core == side))
        carries = jnp.logical_or(root, mine[q])
        forks.append([])
        for d in range(4):
            step = STEP[(d + q) % 4]
            flag = both(carries, member(place, SENDS[d]))
            forks[q].append((flag, chip_at(step, side)))
            expected = expected + number(flag)
            back = (4 - step[0]) % 4, (4 - step[1]) % 4

            @pl.when(both(mine[q], member(place, TAKES[d])))
            def _():
                source, at = chip_at(back, side)
                greet((jnp.where(source < 2, 0, source), at))

        depth.append(sum(number(member(place, DEPTHS[k])) * k for k in range(1, 6)))

    greet(sibling)

    @pl.when(both(z > 0, z < 5))
    def _():
        greet(down)

    @pl.when(z > 4)
    def _():
        greet(up)

    pl.semaphore_wait(barrier, expected)

    def remote(src, dst, send_sem, recv_sem, device):
        return pltpu.make_async_remote_copy(
            src_ref=src, dst_ref=dst, send_sem=send_sem, recv_sem=recv_sem, device_id=device, device_id_type=MESH
        )

    def start(flag, copy):
        @pl.when(flag)
        def _():
            copy.start()

    def finish(flag, part, send_sem, recv_sem):
        @pl.when(flag)
        def _():
            remote(part, part, send_sem, recv_sem, sibling).wait_send()

    def await_part(part, send_sem, recv_sem):
        remote(part, part, send_sem, recv_sem, sibling).wait_recv()

    def c_part(i):
        return pl.ds(pl.multiple_of(i * NB, NB), NB), slice(0, B)

    def r_part(q, j):
        return pl.ds(pl.multiple_of(j * NB, NB), NB), slice(q * width, (q + 1) * width)

    @pl.when(z == 0)
    def _():
        @pl.loop(0, nc)
        def _(i):
            pltpu.make_async_copy(d_ref.at[c_part(i)], c_ref.at[c_part(i)], crecv.at[i]).start()

    @pl.when(root)
    def _():
        @pl.loop(0, n)
        def _(j):
            for q in range(4):
                part = r_part(q, j)
                pltpu.make_async_copy(d_ref.at[part], r_ref.at[part], rrecv.at[q, j]).start()

    def take_c(i):
        part = c_ref.at[c_part(i)]
        await_part(part, csend.at[i, 0], crecv.at[i])
        start(plus, remote(part, part, csend.at[i, 0], crecv.at[i], up))
        start(minus, remote(part, part, csend.at[i, 1], crecv.at[i], down))

        @pl.when(both(root, i < n))
        def _():
            pltpu.make_async_copy(part, p_ref.at[c_part(i)], precv.at[i]).start()

    def take_r(q, j):
        part = r_ref.at[r_part(q, j)]
        await_part(part, rsend.at[q, j, 0], rrecv.at[q, j])
        for d, (flag, device) in enumerate(forks[q]):
            start(flag, remote(part, part, rsend.at[q, j, d], rrecv.at[q, j], device))
        remote(part, part, rsend.at[q, j, 4], rrecv.at[q, j], sibling).start()

    def take_p(i):
        part = p_ref.at[c_part(i)]
        await_part(part, psend.at[i, 0], precv.at[i])
        for d, (flag, device) in enumerate(forks[i % 4]):
            start(flag, remote(part, part, psend.at[i, d], precv.at[i], device))
        remote(part, part, psend.at[i, 4], precv.at[i], sibling).start()

    carrying = [jnp.logical_or(root, mine[q]) for q in range(4)]

    reach = jnp.where(z < 5, z, 8 - z)

    @pl.loop(0, 5 * HOP + 4 * HOP + 3 * nc // 2 + 2)
    def _(t):
        u = t - HOP * reach
        i = (2 * u + u % 3) // 3

        @pl.when(both(u >= 0, u % 3 < 2, i < nc))
        def _():
            take_c(i)

        for i in range(n):

            @pl.when(both(carrying[i % 4], u == 3 * i // 2 + 1 + HOP * depth[i % 4]))
            def _():
                take_p(i)

        for q in range(4):
            j = t - HOP * depth[q]

            @pl.when(both(carrying[q], j >= 0, j < n))
            def _():
                take_r(q, j)

    @pl.loop(0, n)
    def _(j):
        for q in range(4):
            part = r_ref.at[r_part(q, j)]

            @pl.when(jnp.logical_not(carrying[q]))
            def _():
                await_part(part, rsend.at[q, j, 0], rrecv.at[q, j])

            for d in range(4):
                finish(forks[q][d][0], part, rsend.at[q, j, d], rrecv.at[q, j])
            finish(carrying[q], part, rsend.at[q, j, 4], rrecv.at[q, j])

    @pl.loop(0, nc)
    def _(i):
        part = c_ref.at[c_part(i)]
        finish(plus, part, csend.at[i, 0], crecv.at[i])
        finish(minus, part, csend.at[i, 1], crecv.at[i])

    for i in range(n):
        q = i % 4
        part = p_ref.at[c_part(i)]

        @pl.when(jnp.logical_not(carrying[q]))
        def _():
            await_part(part, psend.at[i, 0], precv.at[i])

        for d in range(4):
            finish(forks[q][d][0], part, psend.at[i, d], precv.at[i])
        finish(carrying[q], part, psend.at[i, 4], precv.at[i])


def gather(distances):
    rows, cols = distances.shape
    f32 = jnp.float32
    return pl.pallas_call(
        gather_kernel,
        out_shape=(
            jax.ShapeDtypeStruct((rows, B), f32),
            jax.ShapeDtypeStruct((B, cols), f32),
            jax.ShapeDtypeStruct((B, B), f32),
        ),
        in_specs=[pl.BlockSpec(memory_space=pl.ANY)],
        out_specs=[pl.BlockSpec(memory_space=pltpu.VMEM)] * 3,
        scratch_shapes=[
            pltpu.SemaphoreType.DMA((rows // NB, 2)),
            pltpu.SemaphoreType.DMA((rows // NB,)),
            pltpu.SemaphoreType.DMA((4, B // NB, 5)),
            pltpu.SemaphoreType.DMA((4, B // NB)),
            pltpu.SemaphoreType.DMA((B // NB, 5)),
            pltpu.SemaphoreType.DMA((B // NB,)),
        ],
        compiler_params=pltpu.CompilerParams(collective_id=0, has_side_effects=True),
        name="gather",
    )(distances)


def close_and_extend(p_ref, c_ref, z_refs, wide_refs, panel_refs, old_ref, square_ref, hot_ref):
    strips = len(z_refs)
    left_strips = B // 128
    for r in range(0, B, 128):
        for t in range(left_strips):
            z_refs[t][r : r + 128, :] = p_ref[t * 128 : t * 128 + 128, r : r + 128].T
        for t in range(strips - left_strips):
            z_refs[left_strips + t][r : r + 128, :] = c_ref[t * 128 : t * 128 + 128, r : r + 128].T
    rows = lax.broadcasted_iota(jnp.int32, (B, 128), 0) % 128
    for l in range(KB):
        hot_ref[:, l * 128 : l * 128 + 128] = jnp.where(rows == l, 1.0, 0.0).astype(jnp.bfloat16)

    def lanes(t):
        return slice(t * 128, t * 128 + 128)

    def spread(ref, row, t):
        view = ref.at[row // 8 * 8 : row // 8 * 8 + 8, lanes(t)]
        line = view[pl.ds(row % 8, 8, stride=0), :]
        return jnp.concatenate([line] * (KB // 8), 0)

    def block(k):
        return pl.ds(pl.multiple_of(k, KB), KB)

    def turn(value, k):
        return pltpu.roll(value, lax.rem(128 - lax.rem(k, 128), 128), 1)

    def widen(slot, k, first):
        column = turn(z_refs[first][...], k)
        high = jnp.floor(column * (1 / 32)) * 32
        split = jnp.concatenate([high, column - high], 1).astype(jnp.bfloat16)
        for c in range(0, KB * 128, 512):
            wide_refs[slot][:, c : c + 512] = jnp.dot(split, hot_ref[:, c : c + 512], preferred_element_type=jnp.float32)

    def close(slot, k, first, tiles):
        square = turn(old_ref[:, lanes(first)], k)
        for step in range(KB.bit_length() - 1):
            square_ref[step] = square
            left = square[:, :KB]
            for l in range(KB):
                square = jnp.minimum(square, left[:, l : l + 1] + spread(square_ref.at[step], l, 0))
        values = [old_ref[:, lanes(t)] for t in tiles]
        for l in range(KB):
            column = jnp.broadcast_to(square[:, l : l + 1], (KB, 128))
            values = [jnp.minimum(v, column + spread(old_ref, l, t)) for v, t in zip(values, tiles)]
        for v, t in zip(values, tiles):
            panel_refs[slot][:, lanes(t)] = v

    def through(slot, starts, tiles):
        values = [[z_refs[t][block(r), :] for t in tiles] for r in starts]
        for l in range(KB):
            lines = [spread(panel_refs[slot], l, t) for t in tiles]
            for n, r in enumerate(starts):
                column = wide_refs[slot][block(r), lanes(l)]
                values[n] = [jnp.minimum(v, column + line) for v, line in zip(values[n], lines)]
        return values

    def update(slot, starts, tiles):
        for r, row in zip(starts, through(slot, starts, tiles)):
            for t, value in zip(tiles, row):
                z_refs[t][block(r), :] = value

    right = list(range(left_strips, strips))

    def stage(slot, k, first, others):
        after = k + KB
        rest = [lax.rem(after + r, B) for r in range(KB, B - KB, KB)]
        live = [first] + others
        for t, value in zip(live, through(slot, [after], live)[0]):
            old_ref[:, lanes(t)] = value
        update(slot, rest, [first])
        close(1 - slot, after, first, live)
        widen(1 - slot, after, first)
        for r in rest:
            update(slot, [r], others)
        for t in live:
            z_refs[t][block(after), :] = panel_refs[1 - slot][:, lanes(t)]

    def pair(start, first, others):
        def run(i, carry):
            k = start + i * (2 * KB)
            stage(1, k, first, others)
            stage(0, k + KB, first, others)
            return carry

        return run

    widen(0, 0, 0)
    for t in range(strips):
        old_ref[:, lanes(t)] = z_refs[t][0:KB, :]
    close(0, 0, 0, list(range(strips)))
    for t in range(strips):
        z_refs[t][0:KB, :] = panel_refs[0][:, lanes(t)]
    stage(0, 0, 0, [1] + right)
    lax.fori_loop(0, 3, pair(KB, 0, [1] + right), 0)
    lax.fori_loop(0, 4, pair(128 - KB, 1, right), 0)
    for r in range(0, B - KB, KB):
        update(1, [r], right)
    for t in range(strips - left_strips):
        for r in range(0, B, 128):
            c_ref[t * 128 : t * 128 + 128, r : r + 128] = z_refs[left_strips + t][r : r + 128, :].T


TI, TJ, U = 24, 512, 32


def min_plus(x_ref, y_ref, acc_ref, out_ref, wide_ref):
    height, depth = x_ref.shape
    breadth = y_ref.shape[1]
    blocks, strips = height // TI, breadth // TJ
    share = 8 * (-(-(TI // 8) // strips))

    def widen(slot, left, row0, l0):
        for u in range(U):
            wide_ref[slot, l0 + u, row0 : row0 + share, :] = jnp.broadcast_to(left[:, u : u + 1], (share, 128))
        return pltpu.roll(left, 128 - U, 1)

    for s in range(TI // share):
        for half in range(depth // 128):

            def first(g, left):
                return widen(0, left, s * share, pl.multiple_of(half * 128 + g * U, U))

            lax.fori_loop(0, 128 // U, first, x_ref[s * share : (s + 1) * share, half * 128 : half * 128 + 128])

    def block(b, carry):
        slot = lax.rem(b, 2)
        row0 = pl.multiple_of(b * TI, TI)
        next0 = pl.multiple_of(jnp.minimum(b + 1, blocks - 1) * TI, TI)
        for s in range(strips):
            strip = slice(s * TJ, (s + 1) * TJ)
            value = acc_ref[pl.ds(row0, TI), strip]
            for half in range(depth // 128):

                def group(g, state):
                    value, left = state
                    l0 = pl.multiple_of(half * 128 + g * U, U)
                    right = y_ref.at[pl.ds(l0, U), strip]
                    for u in range(U):
                        wide = wide_ref[slot, l0 + u]
                        row = right[pl.ds(u, 8, stride=0), :]
                        value = jnp.concatenate(
                            [
                                jnp.minimum(
                                    value[:, c : c + 128], wide + jnp.concatenate([row[:, c : c + 128]] * (TI // 8), 0)
                                )
                                for c in range(0, TJ, 128)
                            ],
                            1,
                        )
                    if s * share < TI:
                        left = widen(1 - slot, left, s * share, l0)
                    return value, left

                left = x_ref[pl.ds(next0 + s * share, share), half * 128 : half * 128 + 128]
                value, left = lax.fori_loop(0, 128 // U, group, (value, left))
            out_ref[pl.ds(row0, TI), strip] = value
        return carry

    lax.fori_loop(0, blocks, block, 0)


def update_kernel(c_ref, r_ref, p_ref, d_ref, out_ref, x_ref, old_ref, square_ref, hot_ref, wide_ref, *more):
    x_ref[...] = c_ref[...]
    close_and_extend(p_ref, x_ref, more[4:], more[:2], more[2:4], old_ref, square_ref, hot_ref)
    min_plus(x_ref, r_ref, d_ref, out_ref, wide_ref)


def scratch(rows):
    f32 = jnp.float32
    width = B + rows
    return [
        pltpu.VMEM((rows, B), f32),
        pltpu.VMEM((KB, width), f32),
        pltpu.VMEM((KB.bit_length(), KB, 128), f32),
        pltpu.VMEM((B, KB * 128), jnp.bfloat16),
        pltpu.VMEM((2, B, TI, 128), f32),
        *[pltpu.VMEM((B, KB * 128), f32)] * 2,
        *[pltpu.VMEM((KB, width), f32)] * 2,
        *[pltpu.VMEM((B, 128), f32)] * (width // 128),
    ]


def on_device(distances):
    rows, cols = distances.shape
    f32 = jnp.float32
    c, r, p = gather(distances)
    return pl.pallas_call(
        update_kernel,
        out_shape=jax.ShapeDtypeStruct((rows, cols), f32),
        in_specs=[pl.BlockSpec(memory_space=pltpu.VMEM)] * 4,
        out_specs=pl.BlockSpec(memory_space=pltpu.VMEM),
        scratch_shapes=scratch(rows),
        name="update",
    )(c, r, p, distances)


def solution(mesh):
    spec = P("row", "col")
    return jax.shard_map(on_device, mesh=mesh, in_specs=(spec,), out_specs=spec, check_vma=False)
```

time: 137 us -> 116 us (0.85)
  the two profiles are of different devices: /device:TPU:141 before, /device:TPU:20 now
where the time goes in v3:
time: 116 us
  Pallas kernels  116 us (100%)
    pallas_call x1, Pallas kernels, on_device(): pl.pallas_call(update_kernel, out_shape=jax.ShapeDtypeStruct((rows, cols)...  76.3 us
    pallas_call x1, Pallas kernels, gather(): pl.pallas_call(gather_kernel, out_shape=(jax.ShapeDtypeStruct((rows, B),...  39.6 us

profile of v3, /device:TPU:20, one launch (start us, length us, event | category | flops | bytes accessed | tf_op | source)
XLA Modules:
  0.0 115.9 jit_solution(11479957748205889324)
XLA Ops:
  0.0 39.6 %gather.1 = (f32[384,256]{1,0:T(8,128)}, f32[256,1536]{1,0:T(8,128)}, f32[256,256]{1,0:T(8,128)}) custom-call(f32[384,1536]{1,0:T(8,128)} %d_ref.3), custom_call_target="tpu_custom_call" | custom-call | tf_op jit(solution)/shard_map/gather/pallas_call | solution.py:210
  39.6 76.3 %update.1 = f32[384,1536]{1,0:T(8,128)} custom-call(f32[384,256]{1,0:T(8,128)} %get-tuple-element.8.c_ref, f32[256,1536]{1,0:T(8,128)} %get-tuple-element.9.r_ref, f32[256,256]{1,0:T(8,128)} %get-tuple-element.10.p_ref, f32[384,1536]{1,0:T(8,128)} %d_ref.3), custom_call_target="tpu_custom_call" | custom-call | tf_op jit(solution)/shard_map/update/pallas_call | solution.py:418

commit v4 on v3

--- a/solution.py
+++ b/solution.py
@@ -8,14 +8,15 @@
 from jax.sharding import PartitionSpec as P
 
 B = 256
-NB = 32
+NB = 64
 KB = 16
 MESH = pl.DeviceIdType.MESH
 STEP = ((1, 0), (0, 1), (3, 0), (0, 3))
 SENDS = ((0, 4, 5, 6, 8, 9, 10, 11), (4, 5), (5, 6, 7), (4, 8))
 DEPTHS = ((0,), (4,), (5, 7, 8), (1, 6, 9, 3, 11, 12), (2, 10, 13, 15), (14,))
 TAKES = ((4, 8, 9, 10, 12, 13, 14, 15), (5, 6), (1, 2, 3), (7, 11))
-HOP = 4
+HOP = 3
+P_SLOT = 2
 
 
 def member(value, items):
@@ -73,6 +74,18 @@
         depth.append(sum(number(member(place, DEPTHS[k])) * k for k in range(1, 6)))
 
     greet(sibling)
+    front = core == 0
+    expected = expected + number(front) * 15 + number(both(front, z == 0)) * 7
+
+    @pl.when(front)
+    def _():
+        @pl.loop(1, 16)
+        def _(i):
+            greet((2 * ((chip + i) % 16), z))
+
+        @pl.when(z > 0)
+        def _():
+            greet((row, 0))
 
     @pl.when(both(z > 0, z < 5))
     def _():
@@ -107,6 +120,19 @@
 
     def r_part(q, j):
         return pl.ds(pl.multiple_of(j * NB, NB), NB), slice(q * width, (q + 1) * width)
+
+    piece = B // 16
+
+    def p_part(i):
+        return pl.ds(pl.multiple_of(i * piece, piece), piece), slice(0, B)
+
+    @pl.when(both(root, z == 0))
+    def _():
+        @pl.loop(1, 16)
+        def _(i):
+            remote(d_ref.at[p_part(i)], p_ref.at[p_part(i)], psend.at[0, i], precv.at[i], (2 * i, 0)).start()
+
+        pltpu.make_async_copy(d_ref.at[p_part(0)], p_ref.at[p_part(0)], precv.at[0]).start()
 
     @pl.when(z == 0)
     def _():
@@ -127,10 +153,6 @@
         await_part(part, csend.at[i, 0], crecv.at[i])
         start(plus, remote(part, part, csend.at[i, 0], crecv.at[i], up))
         start(minus, remote(part, part, csend.at[i, 1], crecv.at[i], down))
-
-        @pl.when(both(root, i < n))
-        def _():
-            pltpu.make_async_copy(part, p_ref.at[c_part(i)], precv.at[i]).start()
 
     def take_r(q, j):
         part = r_ref.at[r_part(q, j)]
@@ -139,38 +161,57 @@
             start(flag, remote(part, part, rsend.at[q, j, d], rrecv.at[q, j], device))
         remote(part, part, rsend.at[q, j, 4], rrecv.at[q, j], sibling).start()
 
-    def take_p(i):
-        part = p_ref.at[c_part(i)]
-        await_part(part, psend.at[i, 0], precv.at[i])
-        for d, (flag, device) in enumerate(forks[i % 4]):
-            start(flag, remote(part, part, psend.at[i, d], precv.at[i], device))
-        remote(part, part, psend.at[i, 4], precv.at[i], sibling).start()
+    own = p_ref.at[p_part(chip)]
+
+    def share_piece():
+        await_part(own, psend.at[1, 0], precv.at[chip])
+
+        @pl.when(z == 0)
+        def _():
+            @pl.loop(1, 8)
+            def _(i):
+                remote(own, own, psend.at[3, i], precv.at[chip], (row, i)).start()
+
+        @pl.loop(1, 16)
+        def _(i):
+            remote(own, own, psend.at[1, i], precv.at[chip], (2 * ((chip + i) % 16), z)).start()
+
+        remote(own, own, psend.at[2, 0], precv.at[chip], sibling).start()
+
+    def pass_piece(i):
+        part = p_ref.at[p_part((chip + i) % 16)]
+        await_part(part, psend.at[2, i], precv.at[(chip + i) % 16])
+        remote(part, part, psend.at[2, i], precv.at[(chip + i) % 16], sibling).start()
 
     carrying = [jnp.logical_or(root, mine[q]) for q in range(4)]
 
     reach = jnp.where(z < 5, z, 8 - z)
 
-    @pl.loop(0, 5 * HOP + 4 * HOP + 3 * nc // 2 + 2)
+    @pl.loop(0, max(5 * HOP + n, 4 * HOP + 3 * nc // 2 + 1))
     def _(t):
         u = t - HOP * reach
         i = (2 * u + u % 3) // 3
 
+        @pl.when(both(front, t == jnp.where(z == 0, 0, P_SLOT)))
+        def _():
+            share_piece()
+
         @pl.when(both(u >= 0, u % 3 < 2, i < nc))
         def _():
             take_c(i)
 
-        for i in range(n):
-
-            @pl.when(both(carrying[i % 4], u == 3 * i // 2 + 1 + HOP * depth[i % 4]))
-            def _():
-                take_p(i)
-
         for q in range(4):
             j = t - HOP * depth[q]
 
             @pl.when(both(carrying[q], j >= 0, j < n))
             def _():
                 take_r(q, j)
+
+    @pl.when(front)
+    def _():
+        @pl.loop(1, 16)
+        def _(i):
+            pass_piece(i)
 
     @pl.loop(0, n)
     def _(j):
@@ -191,17 +232,35 @@
         finish(plus, part, csend.at[i, 0], crecv.at[i])
         finish(minus, part, csend.at[i, 1], crecv.at[i])
 
-    for i in range(n):
-        q = i % 4
-        part = p_ref.at[c_part(i)]
-
-        @pl.when(jnp.logical_not(carrying[q]))
-        def _():
-            await_part(part, psend.at[i, 0], precv.at[i])
-
-        for d in range(4):
-            finish(forks[q][d][0], part, psend.at[i, d], precv.at[i])
-        finish(carrying[q], part, psend.at[i, 4], precv.at[i])
+    @pl.when(both(front, root, z == 0))
+    def _():
+        @pl.loop(1, 16)
+        def _(i):
+            part = p_ref.at[p_part(i)]
+            remote(part, part, psend.at[0, i], precv.at[i], sibling).wait_send()
+
+    @pl.when(both(front, z == 0))
+    def _():
+        @pl.loop(1, 8)
+        def _(i):
+            remote(own, own, psend.at[3, i], precv.at[chip], sibling).wait_send()
+
+    @pl.when(front)
+    def _():
+        @pl.loop(1, 16)
+        def _(i):
+            remote(own, own, psend.at[1, i], precv.at[chip], sibling).wait_send()
+
+        @pl.loop(0, 16)
+        def _(i):
+            remote(own, own, psend.at[2, i], precv.at[chip], sibling).wait_send()
+
+    @pl.when(jnp.logical_not(front))
+    def _():
+        @pl.loop(0, 16)
+        def _(i):
+            part = p_ref.at[p_part(i)]
+            await_part(part, psend.at[0, 0], precv.at[i])
 
 
 def gather(distances):
@@ -221,8 +280,8 @@
             pltpu.SemaphoreType.DMA((rows // NB,)),
             pltpu.SemaphoreType.DMA((4, B // NB, 5)),
             pltpu.SemaphoreType.DMA((4, B // NB)),
-            pltpu.SemaphoreType.DMA((B // NB, 5)),
-            pltpu.SemaphoreType.DMA((B // NB,)),
+            pltpu.SemaphoreType.DMA((4, 16)),
+            pltpu.SemaphoreType.DMA((16,)),
         ],
         compiler_params=pltpu.CompilerParams(collective_id=0, has_side_effects=True),
         name="gather",
@@ -334,7 +393,7 @@
 TI, TJ, U = 24, 512, 32
 
 
-def min_plus(x_ref, y_ref, acc_ref, out_ref, wide_ref):
+def min_plus(x_ref, y_ref, acc_ref, wide_ref, finished):
     height, depth = x_ref.shape
     breadth = y_ref.shape[1]
     blocks, strips = height // TI, breadth // TJ
@@ -384,19 +443,36 @@
 
                 left = x_ref[pl.ds(next0 + s * share, share), half * 128 : half * 128 + 128]
                 value, left = lax.fori_loop(0, 128 // U, group, (value, left))
-            out_ref[pl.ds(row0, TI), strip] = value
+            acc_ref[pl.ds(row0, TI), strip] = value
+        finished(pl.ds(row0, TI), b)
         return carry
 
     lax.fori_loop(0, blocks, block, 0)
 
 
-def update_kernel(c_ref, r_ref, p_ref, d_ref, out_ref, x_ref, old_ref, square_ref, hot_ref, wide_ref, *more):
+def update_kernel(
+    c_ref, p_ref, r_hbm, d_hbm, out_hbm, x_ref, old_ref, square_ref, hot_ref, wide_ref, r_ref, d_ref, sem, out_sem, *more
+):
+    r_copy = pltpu.make_async_copy(r_hbm, r_ref, sem.at[0])
+    d_copy = pltpu.make_async_copy(d_hbm, d_ref, sem.at[1])
+    r_copy.start()
+    d_copy.start()
     x_ref[...] = c_ref[...]
     close_and_extend(p_ref, x_ref, more[4:], more[:2], more[2:4], old_ref, square_ref, hot_ref)
-    min_plus(x_ref, r_ref, d_ref, out_ref, wide_ref)
-
-
-def scratch(rows):
+    r_copy.wait()
+    d_copy.wait()
+
+    def put(rows, b):
+        return pltpu.make_async_copy(d_ref.at[rows, :], out_hbm.at[rows, :], out_sem.at[b])
+
+    min_plus(x_ref, r_ref, d_ref, wide_ref, lambda rows, b: put(rows, b).start())
+
+    @pl.loop(0, d_ref.shape[0] // TI)
+    def _(b):
+        put(pl.ds(pl.multiple_of(b * TI, TI), TI), b).wait()
+
+
+def scratch(rows, cols):
     f32 = jnp.float32
     width = B + rows
     return [
@@ -405,6 +481,10 @@
         pltpu.VMEM((KB.bit_length(), KB, 128), f32),
         pltpu.VMEM((B, KB * 128), jnp.bfloat16),
         pltpu.VMEM((2, B, TI, 128), f32),
+        pltpu.VMEM((B, cols), f32),
+        pltpu.VMEM((rows, cols), f32),
+        pltpu.SemaphoreType.DMA((2,)),
+        pltpu.SemaphoreType.DMA((rows // TI,)),
         *[pltpu.VMEM((B, KB * 128), f32)] * 2,
         *[pltpu.VMEM((KB, width), f32)] * 2,
         *[pltpu.VMEM((B, 128), f32)] * (width // 128),
@@ -418,11 +498,11 @@
     return pl.pallas_call(
         update_kernel,
         out_shape=jax.ShapeDtypeStruct((rows, cols), f32),
-        in_specs=[pl.BlockSpec(memory_space=pltpu.VMEM)] * 4,
-        out_specs=pl.BlockSpec(memory_space=pltpu.VMEM),
-        scratch_shapes=scratch(rows),
+        in_specs=[pl.BlockSpec(memory_space=pltpu.VMEM)] * 2 + [pl.BlockSpec(memory_space=pl.ANY)] * 2,
+        out_specs=pl.BlockSpec(memory_space=pl.ANY),
+        scratch_shapes=scratch(rows, cols),
         name="update",
-    )(c, r, p, distances)
+    )(c, p, r, distances)
 
 
 def solution(mesh):

time: 116 us -> 110 us (0.948)
  the two profiles are of different devices: /device:TPU:20 before, /device:TPU:61 now
where the time goes in v4:
time: 110 us; the launch traced here: 109 us
  Pallas kernels  109 us (99%)
    pallas_call x1, Pallas kernels, on_device(): pl.pallas_call(update_kernel, out_shape=jax.ShapeDtypeStruct((rows, cols)...  74.5 us
    pallas_call x1, Pallas kernels, gather(): pl.pallas_call(gather_kernel, out_shape=(jax.ShapeDtypeStruct((rows, B),...  34.9 us

profile of v4, /device:TPU:61, one launch (start us, length us, event | category | flops | bytes accessed | tf_op | source)
XLA Modules:
  0.0 109.4 jit_solution(3759766727314364100)
XLA Ops:
  0.0 34.9 %gather.1 = (f32[384,256]{1,0:T(8,128)}, f32[256,1536]{1,0:T(8,128)}, f32[256,256]{1,0:T(8,128)}) custom-call(f32[384,1536]{1,0:T(8,128)} %d_hbm.1), custom_call_target="tpu_custom_call" | custom-call | tf_op jit(solution)/shard_map/gather/pallas_call | solution.py:269
  34.9 74.5 %update.1 = f32[384,1536]{1,0:T(8,128)} custom-call(f32[384,256]{1,0:T(8,128)} %get-tuple-element.8.c_ref, f32[256,256]{1,0:T(8,128)} %get-tuple-element.9.p_ref, f32[256,1536]{1,0:T(8,128)} %get-tuple-element.10.r_hbm, f32[384,1536]{1,0:T(8,128)} %d_hbm.1), custom_call_target="tpu_custom_call" | custom-call | tf_op jit(solution)/shard_map/update/pallas_call | solution.py:498

commit v5 on v4

--- a/solution.py
+++ b/solution.py
@@ -321,13 +321,15 @@
         for c in range(0, KB * 128, 512):
             wide_refs[slot][:, c : c + 512] = jnp.dot(split, hot_ref[:, c : c + 512], preferred_element_type=jnp.float32)
 
-    def close(slot, k, first, tiles):
+    def close(slot, k, first, tiles, beside=None):
         square = turn(old_ref[:, lanes(first)], k)
         for step in range(KB.bit_length() - 1):
             square_ref[step] = square
             left = square[:, :KB]
             for l in range(KB):
                 square = jnp.minimum(square, left[:, l : l + 1] + spread(square_ref.at[step], l, 0))
+            if beside is not None:
+                square = jnp.minimum(square, beside(step) + 8192.0)
         values = [old_ref[:, lanes(t)] for t in tiles]
         for l in range(KB):
             column = jnp.broadcast_to(square[:, l : l + 1], (KB, 128))
@@ -348,6 +350,7 @@
         for r, row in zip(starts, through(slot, starts, tiles)):
             for t, value in zip(tiles, row):
                 z_refs[t][block(r), :] = value
+        return value
 
     right = list(range(left_strips, strips))
 
@@ -358,9 +361,14 @@
         for t, value in zip(live, through(slot, [after], live)[0]):
             old_ref[:, lanes(t)] = value
         update(slot, rest, [first])
-        close(1 - slot, after, first, live)
+
+        def beside(step):
+            tokens = [update(slot, [r], others) for r in rest[3 * step : 3 * step + 3]]
+            return functools.reduce(jnp.minimum, tokens)
+
         widen(1 - slot, after, first)
-        for r in rest:
+        close(1 - slot, after, first, live, beside)
+        for r in rest[3 * (KB.bit_length() - 1) :]:
             update(slot, [r], others)
         for t in live:
             z_refs[t][block(after), :] = panel_refs[1 - slot][:, lanes(t)]

time: 110 us -> 107 us (0.973)
  Pallas kernels: 109 us -> 107 us
    pallas_call x1, Pallas kernels: 74.5 us -> 72 us  [on_device(): pl.pallas_call(update_kernel, out_shape=jax.ShapeDtypeStruct((rows, cols)...]
where the time goes in v5:
time: 107 us
  Pallas kernels  107 us (100%)
    pallas_call x1, Pallas kernels, on_device(): pl.pallas_call(update_kernel, out_shape=jax.ShapeDtypeStruct((rows, cols)...  72 us
    pallas_call x1, Pallas kernels, gather(): pl.pallas_call(gather_kernel, out_shape=(jax.ShapeDtypeStruct((rows, B),...  34.9 us

profile of v5, /device:TPU:61, one launch (start us, length us, event | category | flops | bytes accessed | tf_op | source)
XLA Modules:
  0.0 106.9 jit_solution(10208191094928596100)
XLA Ops:
  0.0 34.9 %gather.1 = (f32[384,256]{1,0:T(8,128)}, f32[256,1536]{1,0:T(8,128)}, f32[256,256]{1,0:T(8,128)}) custom-call(f32[384,1536]{1,0:T(8,128)} %d_hbm.1), custom_call_target="tpu_custom_call" | custom-call | tf_op jit(solution)/shard_map/gather/pallas_call | solution.py:269
  34.9 72.0 %update.1 = f32[384,1536]{1,0:T(8,128)} custom-call(f32[384,256]{1,0:T(8,128)} %get-tuple-element.8.c_ref, f32[256,256]{1,0:T(8,128)} %get-tuple-element.9.p_ref, f32[256,1536]{1,0:T(8,128)} %get-tuple-element.10.r_hbm, f32[384,1536]{1,0:T(8,128)} %d_hbm.1), custom_call_target="tpu_custom_call" | custom-call | tf_op jit(solution)/shard_map/update/pallas_call | solution.py:506

commit v6 on v5

--- a/solution.py
+++ b/solution.py
@@ -398,27 +398,26 @@
             c_ref[t * 128 : t * 128 + 128, r : r + 128] = z_refs[left_strips + t][r : r + 128, :].T
 
 
-TI, TJ, U = 24, 512, 32
+TI, TJ, U = 16, 768, 32
 
 
 def min_plus(x_ref, y_ref, acc_ref, wide_ref, finished):
     height, depth = x_ref.shape
     breadth = y_ref.shape[1]
     blocks, strips = height // TI, breadth // TJ
-    share = 8 * (-(-(TI // 8) // strips))
-
-    def widen(slot, left, row0, l0):
-        for u in range(U):
-            wide_ref[slot, l0 + u, row0 : row0 + share, :] = jnp.broadcast_to(left[:, u : u + 1], (share, 128))
+    share = U // strips
+
+    def widen(slot, left, l0, columns):
+        for u in columns:
+            wide_ref[slot, l0 + u] = jnp.broadcast_to(left[:, u : u + 1], (TI, 128))
         return pltpu.roll(left, 128 - U, 1)
 
-    for s in range(TI // share):
-        for half in range(depth // 128):
-
-            def first(g, left):
-                return widen(0, left, s * share, pl.multiple_of(half * 128 + g * U, U))
-
-            lax.fori_loop(0, 128 // U, first, x_ref[s * share : (s + 1) * share, half * 128 : half * 128 + 128])
+    for half in range(depth // 128):
+
+        def first(g, left):
+            return widen(0, left, pl.multiple_of(half * 128 + g * U, U), range(U))
+
+        lax.fori_loop(0, 128 // U, first, x_ref[0:TI, half * 128 : half * 128 + 128])
 
     def block(b, carry):
         slot = lax.rem(b, 2)
@@ -445,11 +444,10 @@
                             ],
                             1,
                         )
-                    if s * share < TI:
-                        left = widen(1 - slot, left, s * share, l0)
+                    left = widen(1 - slot, left, l0, range(s * share, s * share + share))
                     return value, left
 
-                left = x_ref[pl.ds(next0 + s * share, share), half * 128 : half * 128 + 128]
+                left = x_ref[pl.ds(next0, TI), half * 128 : half * 128 + 128]
                 value, left = lax.fori_loop(0, 128 // U, group, (value, left))
             acc_ref[pl.ds(row0, TI), strip] = value
         finished(pl.ds(row0, TI), b)

time: 107 us -> 104 us (0.972)
  Pallas kernels: 107 us -> 104 us
    pallas_call x1, Pallas kernels: 72 us -> 69.3 us  [on_device(): pl.pallas_call(update_kernel, out_shape=jax.ShapeDtypeStruct((rows, cols)...]
where the time goes in v6:
time: 104 us
  Pallas kernels  104 us (100%)
    pallas_call x1, Pallas kernels, on_device(): pl.pallas_call(update_kernel, out_shape=jax.ShapeDtypeStruct((rows, cols)...  69.3 us
    pallas_call x1, Pallas kernels, gather(): pl.pallas_call(gather_kernel, out_shape=(jax.ShapeDtypeStruct((rows, B),...  34.9 us

profile of v6, /device:TPU:61, one launch (start us, length us, event | category | flops | bytes accessed | tf_op | source)
XLA Modules:
  0.0 104.2 jit_solution(6004848001690720375)
XLA Ops:
  0.0 34.9 %gather.1 = (f32[384,256]{1,0:T(8,128)}, f32[256,1536]{1,0:T(8,128)}, f32[256,256]{1,0:T(8,128)}) custom-call(f32[384,1536]{1,0:T(8,128)} %d_hbm.1), custom_call_target="tpu_custom_call" | custom-call | tf_op jit(solution)/shard_map/gather/pallas_call | solution.py:269
  34.9 69.3 %update.1 = f32[384,1536]{1,0:T(8,128)} custom-call(f32[384,256]{1,0:T(8,128)} %get-tuple-element.8.c_ref, f32[256,256]{1,0:T(8,128)} %get-tuple-element.9.p_ref, f32[256,1536]{1,0:T(8,128)} %get-tuple-element.10.r_hbm, f32[384,1536]{1,0:T(8,128)} %d_hbm.1), custom_call_target="tpu_custom_call" | custom-call | tf_op jit(solution)/shard_map/update/pallas_call | solution.py:504
